TPU v7x, 32 devices: a whole 2x2x4 slice. The times are simulated.
32 devices in a mesh: row: 8 (over y, x, core), col: 4 (over z).
Axes of the slice: x: 2, y: 2, z: 4, core: 2. Of those that a mesh axis runs over, the one named last changes fastest.
Arguments:
- ancestor_inverse: float32 [6144, 6144], P('row', 'col'), may hold values from -6 to 6
- factor: float32 [6144, 2560], P('row', 'col'), may hold values from -0.078125 to 0.078125
- diag_inverse: float32 [640, 2560], P('row', 'col'), may hold values from -6 to 6
- widths: int32 [4], replicated, may hold values from 384 to 640
- member: int32 [4, 6144], P(None, 'row'), may hold values 0 or 1
Outputs:
- offdiag: float32 [6144, 2560], P('row', 'col')
- diag_blocks: float32 [640, 2560], P('row', 'col')
All inputs are finite; a program needn't handle non-finite values. No bound on the sum of `member` on one device may be relied on, other than what follows from the above.
Results may differ from a plain program's by a relative error of at most 0.0001.
Values sent between devices are 32-bit elements; how exact they have to be, the bound alone decides.
A program may use at most 128 MiB of HBM per device.

v0:
```python
import jax
import jax.numpy as jnp
from jax import lax
from jax.sharding import PartitionSpec as P

W = 640
NODES = 4


def broadcast(block, axis, holder):
    block = jnp.where(lax.axis_index(axis) == holder, block, jnp.zeros_like(block))
    return lax.psum(block, axis)


def per_device(ancestor_inverse, factor, diag_inverse, widths, member):
    grid_rows = lax.axis_size("row")
    grid_cols = lax.axis_size("col")
    groups = grid_rows // grid_cols
    my_row = lax.axis_index("row")
    my_col = lax.axis_index("col")
    shard_cols = factor.shape[1]
    col_start = my_col * shard_cols
    global_cols = col_start + jnp.arange(shard_cols, dtype=jnp.int32)
    node_of = global_cols // W
    within = global_cols % W
    select = (node_of[:, None] == jnp.arange(NODES, dtype=jnp.int32)[None, :]).astype(jnp.float32)
    width_col = jnp.dot(select, widths.astype(jnp.float32), precision=lax.Precision.HIGHEST)
    col_keep = (within.astype(jnp.float32) < width_col).astype(jnp.float32)
    row_keep = jnp.dot(member.T.astype(jnp.float32), select.T, precision=lax.Precision.HIGHEST)
    mask = row_keep * col_keep[None, :]
    masked = factor * mask
    rows_full = lax.all_gather(masked, "col", axis=1, tiled=True)
    pieces = []
    for offset in range(groups):
        pieces.append(broadcast(rows_full, "row", my_col * groups + offset))
    cols_full = jnp.concatenate(pieces, axis=0)
    partial_product = jnp.dot(
        ancestor_inverse,
        cols_full,
        precision=lax.Precision.HIGHEST,
        preferred_element_type=jnp.float32,
    )
    product = lax.psum_scatter(partial_product, "col", scatter_dimension=1, tiled=True)
    offdiag = -product * mask
    node_start = col_start // W * W
    left = lax.dynamic_slice_in_dim(rows_full, node_start, W, 1)
    local_gram = lax.dot_general(
        left,
        product,
        (((0,), (0,)), ((), ())),
        precision=lax.Precision.HIGHEST,
        preferred_element_type=jnp.float32,
    )
    gram = lax.psum_scatter(local_gram, "row", scatter_dimension=0, tiled=True)
    diag_rows_count = diag_inverse.shape[0]
    local_rows = my_row * diag_rows_count + jnp.arange(diag_rows_count, dtype=jnp.int32)
    inside = (local_rows.astype(jnp.float32)[:, None] < width_col[None, :]).astype(jnp.float32)
    diag_blocks = (diag_inverse + gram) * inside * col_keep[None, :]
    return (offdiag, diag_blocks)


def solution(mesh):
    in_specs = (P("row", "col"), P("row", "col"), P("row", "col"), P(), P(None, "row"))
    out_specs = (P("row", "col"), P("row", "col"))
    return jax.shard_map(
        per_device, mesh=mesh, in_specs=in_specs, out_specs=out_specs, check_vma=False
    )
```

profile of v0, /device:TPU:15, one launch (start us, length us, event | category | flops | bytes accessed | tf_op | source)
XLA Modules:
  0.0 608.0 jit_solution(1386914071417419135)
XLA Ops:
  7.2 0.0 all-gather.2.cloned.1.call-start
  7.2 1.0 convolution_reduce_fusion
  8.3 0.0 copy-start.1
  8.3 2.8 copy.7
  11.1 0.0 copy-done.1
  11.1 3.8 bitcast_multiply_fusion.1
  15.0 0.0 all-gather.2.cloned.1.call-update
  15.0 0.0 all-reduce.3.cloned.1.call-start
  15.1 139.3 %all-gather.2.cloned.1.call-done = f32[768,2560]{0,1:T(8,128)} async-done(((f32[768,640]{0,1:T(8,128)}), f32[768,2560]{0,1:T(8,128)}) %all-gather.2.cloned.1.call-update) | async-done | bytes 7864336 | tf_op jit(solution)/shard_map/all_gather | solution.py:32
  154.4 9.7 %broadcast_select_fusion.1 = (f32[768,2560]{0,1:T(8,128)}, f32[768,2560]{0,1:T(8,128)}) fusion(f32[768,2560]{0,1:T(8,128)} %all-gather.2.cloned.1.call-done, pred[]{:T(512)S(6)} %eq.21, pred[]{:T(512)S(6)} %eq.25), kind=kLoop, calls=%fused_computation.6 | loop fusion | flops 3932160 | bytes 23592962 | tf_op jit(solution)/shard_map/jit(_where)/select_n | solution.py:11
  164.1 0.0 all-reduce.3.cloned.1.call-update
  164.1 0.0 reduce-scatter.3.cloned.1.call-start
  164.2 206.7 %all-reduce.3.cloned.1.call-done = (f32[768,2560]{0,1:T(8,128)}, f32[768,2560]{0,1:T(8,128)}) async-done(((f32[768,2560]{0,1:T(8,128)}, f32[768,2560]{0,1:T(8,128)}), (f32[768,2560]{0,1:T(8,128)}, f32[768,2560]{0,1:T(8,128)})) %all-reduce.3.cloned.1.call-update) | async-done | bytes 15728656 | tf_op jit(solution)/shard_map/psum | solution.py:12
  370.8 45.2 %fusion.4 = f32[768,2560]{0,1:T(8,128)} fusion(f32[768,1536]{1,0:T(8,128)} %param.5, f32[768,2560]{0,1:T(8,128)} %get-tuple-element.4, f32[768,2560]{0,1:T(8,128)} %get-tuple-element.5), kind=kOutput, calls=%fused_computation.4 | convolution fusion | flops 36242718720 | bytes 28311552 | tf_op jit(solution)/shard_map/dot_general | solution.py:37
  416.0 0.0 reduce-scatter.3.cloned.1.call-update
  416.1 0.0 reduce-scatter.5.cloned.1.call-start
  416.1 137.2 %reduce-scatter.3.cloned.1.call-done = f32[768,640]{0,1:T(8,128)} async-done(((f32[768,2560]{0,1:T(8,128)}), f32[768,640]{0,1:T(8,128)}) %reduce-scatter.3.cloned.1.call-update) | async-done | bytes 1966096 | tf_op jit(solution)/shard_map/reduce_scatter | solution.py:43
  553.4 8.2 %fusion.7 = f32[640,640]{1,0:T(8,128)} fusion(f32[768,640]{0,1:T(8,128)} %reduce-scatter.3.cloned.1.call-done, f32[768,2560]{0,1:T(8,128)} %all-gather.2.cloned.1.call-done, s32[]{:T(128)S(6)} %select_n.44), kind=kOutput, calls=%fused_computation.9 | convolution fusion | flops 3774873600 | bytes 5570564 | tf_op jit(solution)/shard_map/dot_general | solution.py:47
  561.5 0.0 reduce-scatter.5.cloned.1.call-update
  561.6 3.1 bitcast_multiply_fusion
  564.7 0.0 copy-start
  564.7 2.9 copy.8
  567.5 32.2 %reduce-scatter.5.cloned.1.call-done = f32[80,640]{1,0:T(8,128)} async-done(((f32[640,640]{1,0:T(8,128)}), f32[80,640]{1,0:T(8,128)}) %reduce-scatter.5.cloned.1.call-update) | async-done | bytes 204816 | tf_op jit(solution)/shard_map/reduce_scatter | solution.py:54
  599.8 0.0 copy-done
  599.8 1.7 select_multiply_fusion
  (3 shorter events, 0.0 us)
Async XLA Ops:
  7.2 147.2 %all-gather.2.cloned.1.call-start = ((), (), s32[]{:S(2)}) async-start(), calls=%async_computation.2 | async-start | bytes 9830400 | tf_op jit(solution)/shard_map/all_gather | solution.py:32
  8.3 2.8 copy-start.1
  15.0 355.9 %all-reduce.3.cloned.1.call-start = ((), (), s32[]{:S(2)}) async-start(), calls=%async_computation.5 | async-start | bytes 31457280 | tf_op jit(solution)/shard_map/psum | solution.py:12
  164.1 389.2 %reduce-scatter.3.cloned.1.call-start = ((), (), s32[]{:S(2)}) async-start(), calls=%async_computation.3 | async-start | bytes 9830400 | tf_op jit(solution)/shard_map/reduce_scatter | solution.py:43
  416.1 183.7 %reduce-scatter.5.cloned.1.call-start = ((), (), s32[]{:S(2)}) async-start(), calls=%async_computation.4 | async-start | bytes 1843200 | tf_op jit(solution)/shard_map/reduce_scatter | solution.py:54
  564.7 35.1 %copy-start = (f32[80,640]{1,0:T(8,128)S(1)}, f32[80,640]{1,0:T(8,128)}, u32[]{:S(2)}) copy-start(f32[80,640]{1,0:T(8,128)} %param.7) | copy-start | bytes 614404
Sparse Core Ops, SparseCore 0:
  15.1 139.2 all-gather.1
  164.3 206.5 all-reduce.2
  416.2 137.1 reduce-scatter.2
  561.7 38.0 reduce-scatter.4
where the time goes:
time: 611 us; the launch traced here: 608 us
  waiting for transfers between devices  515 us (84%)
  matrix products  58.2 us (10%)
  other arithmetic  14.6 us (2%)
  between operations  13.8 us (2%)
    psum x1, waiting for transfers between devices, broadcast(): return lax.psum(block, axis)  207 us
    all_gather x1, waiting for transfers between devices, per_device(): rows_full = lax.all_gather(masked, 'col', axis=1, tiled=True)  139 us
    reduce_scatter x1, waiting for transfers between devices, per_device(): lax.psum_scatter(partial_product, 'col', scatter_dimension=1, tiled=True)  137 us
    dot_general x1, matrix products, per_device(): jnp.dot(ancestor_inverse, cols_full, precision=lax.Precision.HIGHEST, pre...  45.2 us
    reduce_scatter x1, waiting for transfers between devices, per_device(): gram = lax.psum_scatter(local_gram, 'row', scatter_dimension=0, tiled=True)  32.2 us
  transfers between devices with their start and end apart: 4, of which 4 were waited for; matrix products, arithmetic and copies ran while one was open for 1% of the time, Pallas kernels for 0%

commit v1 on v0

v1 whole, which is shorter than its diff:
```python
import functools

import jax
import jax.numpy as jnp
from jax import lax
from jax.experimental import pallas as pl
from jax.experimental.pallas import tpu as pltpu
from jax.sharding import PartitionSpec as P

W = 640
NODES = 4
MESH = pl.DeviceIdType.MESH


def split(x):
    hi = x.astype(jnp.bfloat16)
    lo = (x - hi.astype(jnp.float32)).astype(jnp.bfloat16)
    return hi, lo


def row_tile(rows, most):
    return max(t for t in range(16, most + 1, 16) if rows % t == 0)


def product_kernel(
    R, C, a_ref, l_ref, out_ref, gath, part, recv, a_hi, a_lo, b_hi, b_lo,
    s1, r1, s2, r2, s3, r3, s4, r4,
):
    G = R // C
    half_ring = C // 2
    row = lax.axis_index("row")
    c = lax.axis_index("col")
    j = row // G
    g = lax.rem(row, G)
    rows, cols = l_ref.shape
    chunk = rows // C
    half = rows // 2

    barrier = pltpu.get_barrier_semaphore()

    def greet(r, q):
        pl.semaphore_signal(barrier, inc=1, device_id=(r, q), device_id_type=MESH)

    for n in range(C):
        @pl.when(jnp.logical_or(j != c, j != n))
        def _():
            greet(n * G + g, j)

        @pl.when(jnp.logical_or(j != c, c != n))
        def _():
            greet(c * G + g, n)
    for m in range(1, C):
        greet(lax.rem(j + m, C) * G + g, c)
    for n in range(1, G):
        greet(j * G + lax.rem(g + n, G), c)
    greet(row, lax.rem(c + 1, C))
    greet(row, lax.rem(c + C - 1, C))
    pl.semaphore_wait(barrier, 2 * C + (C - 1) + (G - 1) + 2 - 2 * (j == c).astype(jnp.int32))

    def remote(src, dst, ssem, rsem, r, q):
        return pltpu.make_async_remote_copy(
            src_ref=src, dst_ref=dst, send_sem=ssem, recv_sem=rsem,
            device_id=(r, q), device_id_type=MESH,
        )

    for n in range(C):
        src = l_ref.at[pl.ds(n * chunk, chunk)]
        dst = gath.at[c, g, pl.ds(n * chunk, chunk)]
        own = jnp.logical_and(j == c, j == n)

        @pl.when(jnp.logical_not(own))
        def _():
            remote(src, dst, s1.at[n], r1.at[c], n * G + g, j).start()

        @pl.when(own)
        def _():
            pltpu.make_async_copy(src, dst, r1.at[c]).start()

    ta = row_tile(rows, 128)

    @pl.loop(0, rows // ta)
    def _(t):
        at = pl.ds(pl.multiple_of(t * ta, ta), ta)
        hi, lo = split(a_ref[at, :])
        a_hi[at, :] = hi
        a_lo[at, :] = lo

    order = [(half_ring, 0)]
    for s in range(half_ring - 1, 0, -1):
        order += [(s, -1), (s, 1)]
    order += [(0, 0)]
    blocks = []
    for s, way in order:
        blocks.append(lax.rem(c + (s if way >= 0 else C - s), C))

    mine = pl.ds(pl.multiple_of(j * chunk, chunk), chunk)

    def plane_copy(i, m):
        ref = gath.at[blocks[i], g, mine]
        return remote(ref, ref, s2.at[i, m - 1], r2.at[i, m - 1], lax.rem(j + m, C) * G + g, c)

    def plane_wait(i, m):
        from_j = lax.rem(j + C - m, C)
        ref = gath.at[blocks[i], g, pl.ds(pl.multiple_of(from_j * chunk, chunk), chunk)]
        remote(ref, ref, s2.at[i, m - 1], r2.at[i, m - 1], row, c).wait_recv()

    def group_copy(i, n):
        ref = gath.at[blocks[i], g]
        return remote(ref, ref, s3.at[i, n - 1], r3.at[i, n - 1], j * G + lax.rem(g + n, G), c)

    def group_wait(i, n):
        ref = gath.at[blocks[i], lax.rem(g + G - n, G)]
        remote(ref, ref, s3.at[i, n - 1], r3.at[i, n - 1], row, c).wait_recv()

    for i in range(C):
        q = blocks[i]
        ref = gath.at[q, g, mine]
        remote(ref, ref, s1.at[0], r1.at[q], row, c).wait_recv()
        for m in range(1, C):
            plane_copy(i, m).start()

    tb = row_tile(rows, 128)
    tm = row_tile(rows, 256)

    def multiply(i):
        q = blocks[i]
        for gg in range(G):
            @pl.loop(0, rows // tb)
            def _(t):
                hi, lo = split(gath[q, gg, pl.ds(pl.multiple_of(t * tb, tb), tb), :])
                at = pl.ds(pl.multiple_of(gg * rows + t * tb, tb), tb)
                b_hi[at, :] = hi
                b_lo[at, :] = lo

        @pl.loop(0, rows // tm)
        def _(t):
            at = pl.ds(pl.multiple_of(t * tm, tm), tm)
            dot = functools.partial(jnp.dot, preferred_element_type=jnp.float32)
            x = dot(a_hi[at, :], b_lo[...]) + dot(a_lo[at, :], b_hi[...])
            part[i, at, :] = x + dot(a_hi[at, :], b_hi[...])

    def ring_copy(i, way, s):
        to = lax.rem(c + (C - 1 if way == 0 else 1), C)
        piece = pl.ds(way * half, half) if s == half_ring else pl.ds(0, rows)
        return remote(
            part.at[i, piece], recv.at[way, s - 1, piece],
            s4.at[way, s - 1], r4.at[way, s - 1], row, to,
        )

    def ring_wait(way, s):
        piece = pl.ds(way * half, half) if s + 1 == half_ring else pl.ds(0, rows)
        ref = recv.at[way, s, piece]
        remote(ref, ref, s4.at[way, s], r4.at[way, s], row, c).wait_recv()

    def accumulate(i, way, s):
        lo, n = (way * half, half) if s + 1 == half_ring else (0, rows)
        step = row_tile(n, 128)

        @pl.loop(0, n // step)
        def _(t):
            at = pl.ds(pl.multiple_of(lo + t * step, 16), step)
            part[i, at, :] = part[i, at, :] + recv[way, s, at, :]

    sends = []
    for i, (s, way) in enumerate(order):
        for m in range(1, C):
            plane_wait(i, m)
        for n in range(1, G):
            group_copy(i, n).start()
        for n in range(1, G):
            group_wait(i, n)
        multiply(i)
        if s == half_ring:
            ways = (0, 1)
        elif s:
            ways = (0,) if way < 0 else (1,)
        else:
            ways = ()
        for w in ways:
            if s < half_ring:
                ring_wait(w, s)
                accumulate(i, w, s)
            copy = ring_copy(i, w, s)
            copy.start()
            sends.append(copy)

    ring_wait(0, 0)
    ring_wait(1, 0)

    @pl.loop(0, rows // ta)
    def _(t):
        at = pl.ds(pl.multiple_of(t * ta, ta), ta)
        out_ref[at, :] = part[C - 1, at, :] + recv[0, 0, at, :] + recv[1, 0, at, :]

    for copy in sends:
        copy.wait_send()
    for n in range(C):
        src = l_ref.at[pl.ds(n * chunk, chunk)]

        @pl.when(jnp.logical_or(j != c, j != n))
        def _():
            remote(src, src, s1.at[n], r1.at[0], row, c).wait_send()
    for i in range(C):
        for m in range(1, C):
            plane_copy(i, m).wait_send()
        for n in range(1, G):
            group_copy(i, n).wait_send()


def grid_product(R, C, a, l):
    rows, cols = l.shape
    G = R // C
    depth = a.shape[1]
    vmem = pl.BlockSpec(memory_space=pltpu.VMEM)
    dma = pltpu.SemaphoreType.DMA
    return pl.pallas_call(
        functools.partial(product_kernel, R, C),
        out_shape=jax.ShapeDtypeStruct((rows, cols), jnp.float32),
        in_specs=[vmem, vmem],
        out_specs=vmem,
        scratch_shapes=[
            pltpu.VMEM((C, G, rows, cols), jnp.float32),
            pltpu.VMEM((C, rows, cols), jnp.float32),
            pltpu.VMEM((2, C // 2, rows, cols), jnp.float32),
            pltpu.VMEM((rows, depth), jnp.bfloat16),
            pltpu.VMEM((rows, depth), jnp.bfloat16),
            pltpu.VMEM((depth, cols), jnp.bfloat16),
            pltpu.VMEM((depth, cols), jnp.bfloat16),
            dma((C,)),
            dma((C,)),
            dma((C, C - 1)),
            dma((C, C - 1)),
            dma((C, max(G - 1, 1))),
            dma((C, max(G - 1, 1))),
            dma((2, C // 2)),
            dma((2, C // 2)),
        ],
        compiler_params=pltpu.CompilerParams(
            collective_id=0, has_side_effects=True, vmem_limit_bytes=67043328
        ),
    )(a, l)


def per_device(ancestor_inverse, factor, diag_inverse, widths, member):
    R = lax.axis_size("row")
    C = lax.axis_size("col")
    my_row = lax.axis_index("row")
    my_col = lax.axis_index("col")
    shard_cols = factor.shape[1]
    col_start = my_col * shard_cols
    global_cols = col_start + jnp.arange(shard_cols, dtype=jnp.int32)
    node_of = global_cols // W
    within = global_cols % W
    select = node_of[None, :] == jnp.arange(NODES, dtype=jnp.int32)[:, None]
    width_col = jnp.sum(jnp.where(select, widths[:, None], 0), axis=0)
    col_keep = within < width_col
    pick = jnp.where(select & col_keep[None, :], 1.0, 0.0).astype(jnp.bfloat16)
    mask = lax.dot_general(
        member.astype(jnp.bfloat16), pick, (((0,), (0,)), ((), ())),
        preferred_element_type=jnp.float32,
    )
    masked = factor * mask
    product = grid_product(R, C, ancestor_inverse, masked)
    offdiag = -product * mask
    if shard_cols == W:
        left = masked
    else:
        rows_full = lax.all_gather(masked, "col", axis=1, tiled=True)
        left = lax.dynamic_slice_in_dim(rows_full, col_start // W * W, W, 1)
    local_gram = lax.dot_general(
        left, product, (((0,), (0,)), ((), ())),
        precision=lax.Precision.HIGH, preferred_element_type=jnp.float32,
    )
    gram = lax.psum_scatter(local_gram, "row", scatter_dimension=0, tiled=True)
    diag_rows = diag_inverse.shape[0]
    local_rows = my_row * diag_rows + jnp.arange(diag_rows, dtype=jnp.int32)
    inside = (local_rows[:, None] < width_col[None, :]) & col_keep[None, :]
    diag_blocks = (diag_inverse + gram) * inside.astype(jnp.float32)
    return (offdiag, diag_blocks)


def solution(mesh):
    in_specs = (P("row", "col"), P("row", "col"), P("row", "col"), P(), P(None, "row"))
    out_specs = (P("row", "col"), P("row", "col"))
    return jax.shard_map(
        per_device, mesh=mesh, in_specs=in_specs, out_specs=out_specs, check_vma=False
    )
```

time: 611 us -> 345 us (0.56)
  waiting for transfers between devices: 515 us -> 34.2 us
  Pallas kernels: 0 us -> 278 us
  matrix products: 58.2 us -> 10.2 us
  other arithmetic: 14.6 us -> 5.54 us
    pallas_call x0 -> x1, Pallas kernels: none -> 278 us  [grid_product(): pl.pallas_call(functools.partial(product_kernel, R, C), out_shape=jax.Sha...]
    psum x1 -> x0, waiting for transfers between devices: 207 us -> none  [broadcast(): return lax.psum(block, axis)]
    all_gather x1 -> x0, waiting for transfers between devices: 139 us -> none  [per_device(): rows_full = lax.all_gather(masked, 'col', axis=1, tiled=True)]
    reduce_scatter x1 -> x0, waiting for transfers between devices: 137 us -> none  [per_device(): lax.psum_scatter(partial_product, 'col', scatter_dimension=1, tiled=True)]
    dot_general x3 -> x1, matrix products: 50 us -> 3.95 us  [per_device(): lax.dot_general(member.astype(jnp.bfloat16), pick, (((0,), (0,)), ((), ()...]
    select_n x1 -> x0, other arithmetic: 9.74 us -> none  [broadcast(): jnp.where(lax.axis_index(axis) == holder, block, jnp.zeros_like(block))]
  transfers between devices with their start and end apart: 4 -> 1, of which waited for: 4 -> 1; matrix products, arithmetic and copies ran while one was open for 1% -> 1% of each run, Pallas kernels for 0% -> 0%
where the time goes in v1:
time: 345 us; the launch traced here: 342 us
  Pallas kernels  278 us (81%)
  waiting for transfers between devices  34.2 us (10%)
  between operations  14.1 us (4%)
  matrix products  10.2 us (3%)
  other arithmetic  5.54 us (2%)
    pallas_call x1, Pallas kernels, grid_product(): pl.pallas_call(functools.partial(product_kernel, R, C), out_shape=jax.Sha...  278 us
    reduce_scatter x1, waiting for transfers between devices, per_device(): gram = lax.psum_scatter(local_gram, 'row', scatter_dimension=0, tiled=True)  34.2 us
  transfers between devices with their start and end apart: 1, of which 1 were waited for; matrix products, arithmetic and copies ran while one was open for 1% of the time, Pallas kernels for 0%

profile of v1, /device:TPU:15, one launch (start us, length us, event | category | flops | bytes accessed | tf_op | source)
XLA Modules:
  0.0 342.3 jit_solution(13898960874102837644)
XLA Ops:
  7.2 0.0 reduce-scatter.2.cloned.1.call-start
  7.2 0.7 select_reduce_fusion
  8.0 0.0 copy-start.2
  8.0 0.6 copy-done.2
  8.6 0.0 copy-start.4
  8.6 4.0 %bitcast_multiply_fusion.1 = (f32[768,640]{1,0:T(8,128)}, f32[640,768]{0,1:T(8,128)}) fusion(f32[768,640]{1,0:T(8,128)} %param.6, s32[4,768]{1,0:T(4,128)} %param.9, s32[640]{0:T(1024)S(1)} %add_select_fusion.2, pred[640]{0:T(1024)(128)(4,1)S(1)} %fusion.7), kind=kOutput, calls=%fused_computation.1 | convolution fusion | flops 4436992 | bytes 5913728 | tf_op jit(solution)/shard_map/dot_general | solution.py:258
  12.5 0.0 copy-done.4
  12.5 277.5 %shard_map.68 = f32[768,640]{1,0:T(8,128)} custom-call(f32[768,1536]{1,0:T(8,128)} %a_ref.1, f32[768,640]{1,0:T(8,128)} %get-tuple-element.2.l_ref), custom_call_target="tpu_custom_call" | custom-call | tf_op jit(solution)/shard_map/pallas_call | solution.py:216
  290.1 0.0 copy-start
  290.1 6.3 %fusion.15 = f32[640,640]{1,0:T(8,128)} fusion(f32[768,640]{1,0:T(8,128)} %get-tuple-element.2.l_ref, f32[768,640]{1,0:T(8,128)} %shard_map.68), kind=kOutput, calls=%fused_computation.26 | convolution fusion | flops 1887436800 | bytes 5570560 | tf_op jit(solution)/shard_map/dot_general | solution.py:270
  296.4 0.0 reduce-scatter.2.cloned.1.call-update
  296.4 0.0 copy-done
  296.4 0.0 copy-start.1
  296.4 0.0 copy-start.3
  296.4 0.0 copy-start.5
  296.4 3.1 bitcast_multiply_fusion
  299.5 34.2 %reduce-scatter.2.cloned.1.call-done = f32[80,640]{1,0:T(8,128)} async-done(((f32[640,640]{1,0:T(8,128)}), f32[80,640]{1,0:T(8,128)}) %reduce-scatter.2.cloned.1.call-update) | async-done | bytes 204816 | tf_op jit(solution)/shard_map/reduce_scatter | solution.py:274
  333.7 0.0 copy-done.1
  333.7 0.0 copy-done.3
  333.7 0.0 copy-done.5
  333.7 1.7 add_select_fusion
  (3 shorter events, 0.0 us)
Async XLA Ops:
  7.2 326.6 %reduce-scatter.2.cloned.1.call-start = ((), (), s32[]{:S(2)}) async-start(), calls=%async_computation.1 | async-start | bytes 1843200 | tf_op jit(solution)/shard_map/reduce_scatter | solution.py:274
  8.0 0.6 copy-start.2
  8.6 4.0 %copy-start.4 = (pred[640]{0:T(1024)(128)(4,1)}, pred[640]{0:T(1024)(128)(4,1)S(1)}, u32[]{:S(2)}) copy-start(pred[640]{0:T(1024)(128)(4,1)S(1)} %fusion.7) | copy-start | bytes 1924
  290.1 6.3 %copy-start = (f32[768,640]{1,0:T(8,128)S(1)}, f32[768,640]{1,0:T(8,128)}, u32[]{:S(2)}) copy-start(f32[768,640]{1,0:T(8,128)} %shard_map.68) | copy-start | bytes 5898244
  296.4 37.3 %copy-start.1 = (f32[80,640]{1,0:T(8,128)S(1)}, f32[80,640]{1,0:T(8,128)}, u32[]{:S(2)}) copy-start(f32[80,640]{1,0:T(8,128)} %param.7) | copy-start | bytes 614404
  296.4 37.3 %copy-start.3 = (s32[640]{0:T(1024)S(1)}, s32[640]{0:T(1024)}, u32[]{:S(2)}) copy-start(s32[640]{0:T(1024)} %copy-done.2) | copy-start | bytes 7684
  296.4 37.3 %copy-start.5 = (pred[640]{0:T(1024)(128)(4,1)S(1)}, pred[640]{0:T(1024)(128)(4,1)}, u32[]{:S(2)}) copy-start(pred[640]{0:T(1024)(128)(4,1)} %copy-done.4) | copy-start | bytes 1924
Sparse Core Ops, SparseCore 0:
  296.5 37.1 reduce-scatter.1

commit v2 on v1

--- a/solution.py
+++ b/solution.py
@@ -23,8 +23,8 @@
 
 
 def product_kernel(
-    R, C, a_ref, l_ref, out_ref, gath, part, recv, a_hi, a_lo, b_hi, b_lo,
-    s1, r1, s2, r2, s3, r3, s4, r4,
+    R, C, a_ref, l_ref, left_ref, out_ref, gram_ref, mid, gath, part, recv, gram, inbox,
+    a_hi, a_lo, b_hi, b_lo, s0, r0, s1, r1, s2, r2, s3, r3, s4, r4, s5, r5, own_sem,
 ):
     G = R // C
     half_ring = C // 2
@@ -33,6 +33,7 @@
     j = row // G
     g = lax.rem(row, G)
     rows, cols = l_ref.shape
+    depth = a_ref.shape[1]
     chunk = rows // C
     half = rows // 2
 
@@ -41,21 +42,11 @@
     def greet(r, q):
         pl.semaphore_signal(barrier, inc=1, device_id=(r, q), device_id_type=MESH)
 
-    for n in range(C):
-        @pl.when(jnp.logical_or(j != c, j != n))
-        def _():
-            greet(n * G + g, j)
-
-        @pl.when(jnp.logical_or(j != c, c != n))
-        def _():
-            greet(c * G + g, n)
+    for m in range(1, R):
+        greet(lax.rem(row + m, R), c)
     for m in range(1, C):
-        greet(lax.rem(j + m, C) * G + g, c)
-    for n in range(1, G):
-        greet(j * G + lax.rem(g + n, G), c)
-    greet(row, lax.rem(c + 1, C))
-    greet(row, lax.rem(c + C - 1, C))
-    pl.semaphore_wait(barrier, 2 * C + (C - 1) + (G - 1) + 2 - 2 * (j == c).astype(jnp.int32))
+        greet(row, lax.rem(c + m, C))
+    pl.semaphore_wait(barrier, R + C - 2)
 
     def remote(src, dst, ssem, rsem, r, q):
         return pltpu.make_async_remote_copy(
@@ -63,18 +54,31 @@
             device_id=(r, q), device_id_type=MESH,
         )
 
-    for n in range(C):
-        src = l_ref.at[pl.ds(n * chunk, chunk)]
-        dst = gath.at[c, g, pl.ds(n * chunk, chunk)]
-        own = jnp.logical_and(j == c, j == n)
-
-        @pl.when(jnp.logical_not(own))
-        def _():
-            remote(src, dst, s1.at[n], r1.at[c], n * G + g, j).start()
-
-        @pl.when(own)
-        def _():
-            pltpu.make_async_copy(src, dst, r1.at[c]).start()
+    mine = pl.ds(pl.multiple_of(j * chunk, chunk), chunk)
+
+    def spread_copy(m):
+        n = lax.rem(j + m, C)
+        src = l_ref.at[pl.ds(pl.multiple_of(n * chunk, chunk), chunk)]
+        return remote(src, mid.at[j], s0.at[m - 1], r0.at[m - 1], n * G + g, c)
+
+    def column_copy(p, m):
+        return remote(
+            mid.at[p], gath.at[c, g, mine], s1.at[m - 1], r1.at[m - 1], row, p
+        )
+
+    for m in range(1, C):
+        spread_copy(m).start()
+    own = pltpu.make_async_copy(l_ref.at[mine], mid.at[j], own_sem.at[0])
+    own.start()
+    own.wait()
+    for m in range(1, C):
+        ref = mid.at[lax.rem(j + C - m, C)]
+        remote(ref, ref, s0.at[m - 1], r0.at[m - 1], row, c).wait_recv()
+    ways_on = sorted(range(1, C), key=lambda m: -min(m, C - m))
+    for m in ways_on:
+        column_copy(lax.rem(c + m, C), m).start()
+    keep = pltpu.make_async_copy(mid.at[c], gath.at[c, g, mine], own_sem.at[1])
+    keep.start()
 
     ta = row_tile(rows, 128)
 
@@ -82,8 +86,8 @@
     def _(t):
         at = pl.ds(pl.multiple_of(t * ta, ta), ta)
         hi, lo = split(a_ref[at, :])
-        a_hi[at, :] = hi
-        a_lo[at, :] = lo
+        a_hi[at, pl.ds(0, depth)] = hi
+        a_lo[at, pl.ds(0, depth)] = lo
 
     order = [(half_ring, 0)]
     for s in range(half_ring - 1, 0, -1):
@@ -93,8 +97,6 @@
     for s, way in order:
         blocks.append(lax.rem(c + (s if way >= 0 else C - s), C))
 
-    mine = pl.ds(pl.multiple_of(j * chunk, chunk), chunk)
-
     def plane_copy(i, m):
         ref = gath.at[blocks[i], g, mine]
         return remote(ref, ref, s2.at[i, m - 1], r2.at[i, m - 1], lax.rem(j + m, C) * G + g, c)
@@ -112,10 +114,13 @@
         ref = gath.at[blocks[i], lax.rem(g + G - n, G)]
         remote(ref, ref, s3.at[i, n - 1], r3.at[i, n - 1], row, c).wait_recv()
 
-    for i in range(C):
-        q = blocks[i]
-        ref = gath.at[q, g, mine]
-        remote(ref, ref, s1.at[0], r1.at[q], row, c).wait_recv()
+    for i, (s, way) in enumerate(order):
+        if s:
+            m = C - s if way >= 0 else s
+            ref = gath.at[blocks[i], g, mine]
+            remote(ref, ref, s1.at[m - 1], r1.at[m - 1], row, c).wait_recv()
+        else:
+            keep.wait()
         for m in range(1, C):
             plane_copy(i, m).start()
 
@@ -136,8 +141,9 @@
         def _(t):
             at = pl.ds(pl.multiple_of(t * tm, tm), tm)
             dot = functools.partial(jnp.dot, preferred_element_type=jnp.float32)
-            x = dot(a_hi[at, :], b_lo[...]) + dot(a_lo[at, :], b_hi[...])
-            part[i, at, :] = x + dot(a_hi[at, :], b_hi[...])
+            x_hi, x_lo = a_hi[at, pl.ds(0, depth)], a_lo[at, pl.ds(0, depth)]
+            y_hi, y_lo = b_hi[pl.ds(0, depth), :], b_lo[pl.ds(0, depth), :]
+            part[i, at, :] = dot(x_hi, y_lo) + dot(x_lo, y_hi) + dot(x_hi, y_hi)
 
     def ring_copy(i, way, s):
         to = lax.rem(c + (C - 1 if way == 0 else 1), C)
@@ -190,16 +196,47 @@
     @pl.loop(0, rows // ta)
     def _(t):
         at = pl.ds(pl.multiple_of(t * ta, ta), ta)
-        out_ref[at, :] = part[C - 1, at, :] + recv[0, 0, at, :] + recv[1, 0, at, :]
+        x = part[C - 1, at, :] + recv[0, 0, at, :] + recv[1, 0, at, :]
+        out_ref[at, :] = x
+        hi, lo = split(x)
+        b_hi[at, :] = hi
+        b_lo[at, :] = lo
+        hi, lo = split(left_ref[at, :])
+        a_hi[at, pl.ds(0, W)] = hi
+        a_lo[at, pl.ds(0, W)] = lo
+
+    for t in range(W // 128):
+        at = pl.ds(t * 128, 128)
+        dot = functools.partial(
+            lax.dot_general, dimension_numbers=(((0,), (0,)), ((), ())),
+            preferred_element_type=jnp.float32,
+        )
+        p_hi, p_lo = b_hi[pl.ds(0, rows), :], b_lo[pl.ds(0, rows), :]
+        x = dot(a_hi[:, at], p_lo) + dot(a_lo[:, at], p_hi)
+        gram[at, :] = x + dot(a_hi[:, at], p_hi)
+
+    share = W // R
+
+    def gram_copy(m):
+        to = lax.rem(row + m, R)
+        src = gram.at[pl.ds(pl.multiple_of(to * share, 8), share)]
+        return remote(src, inbox.at[m - 1], s5.at[m - 1], r5.at[m - 1], to, c)
+
+    for m in range(1, R):
+        gram_copy(m).start()
+    total = gram[pl.ds(pl.multiple_of(row * share, 8), share), :]
+    for m in range(1, R):
+        gram_copy(m).wait_recv()
+        total = total + inbox[m - 1]
+    gram_ref[...] = total
 
     for copy in sends:
         copy.wait_send()
-    for n in range(C):
-        src = l_ref.at[pl.ds(n * chunk, chunk)]
-
-        @pl.when(jnp.logical_or(j != c, j != n))
-        def _():
-            remote(src, src, s1.at[n], r1.at[0], row, c).wait_send()
+    for m in range(1, C):
+        spread_copy(m).wait_send()
+        column_copy(lax.rem(c + m, C), m).wait_send()
+    for m in range(1, R):
+        gram_copy(m).wait_send()
     for i in range(C):
         for m in range(1, C):
             plane_copy(i, m).wait_send()
@@ -207,7 +244,7 @@
             group_copy(i, n).wait_send()
 
 
-def grid_product(R, C, a, l):
+def grid_product(R, C, a, l, left):
     rows, cols = l.shape
     G = R // C
     depth = a.shape[1]
@@ -215,30 +252,41 @@
     dma = pltpu.SemaphoreType.DMA
     return pl.pallas_call(
         functools.partial(product_kernel, R, C),
-        out_shape=jax.ShapeDtypeStruct((rows, cols), jnp.float32),
-        in_specs=[vmem, vmem],
-        out_specs=vmem,
+        out_shape=[
+            jax.ShapeDtypeStruct((rows, cols), jnp.float32),
+            jax.ShapeDtypeStruct((W // R, cols), jnp.float32),
+        ],
+        in_specs=[vmem, vmem, vmem],
+        out_specs=[vmem, vmem],
         scratch_shapes=[
+            pltpu.VMEM((C, rows // C, cols), jnp.float32),
             pltpu.VMEM((C, G, rows, cols), jnp.float32),
             pltpu.VMEM((C, rows, cols), jnp.float32),
             pltpu.VMEM((2, C // 2, rows, cols), jnp.float32),
-            pltpu.VMEM((rows, depth), jnp.bfloat16),
-            pltpu.VMEM((rows, depth), jnp.bfloat16),
-            pltpu.VMEM((depth, cols), jnp.bfloat16),
-            pltpu.VMEM((depth, cols), jnp.bfloat16),
-            dma((C,)),
-            dma((C,)),
+            pltpu.VMEM((W, cols), jnp.float32),
+            pltpu.VMEM((R - 1, W // R, cols), jnp.float32),
+            pltpu.VMEM((rows, max(depth, W)), jnp.bfloat16),
+            pltpu.VMEM((rows, max(depth, W)), jnp.bfloat16),
+            pltpu.VMEM((max(depth, rows), cols), jnp.bfloat16),
+            pltpu.VMEM((max(depth, rows), cols), jnp.bfloat16),
+            dma((C - 1,)),
+            dma((C - 1,)),
+            dma((C - 1,)),
+            dma((C - 1,)),
             dma((C, C - 1)),
             dma((C, C - 1)),
             dma((C, max(G - 1, 1))),
             dma((C, max(G - 1, 1))),
             dma((2, C // 2)),
             dma((2, C // 2)),
+            dma((R - 1,)),
+            dma((R - 1,)),
+            dma((2,)),
         ],
         compiler_params=pltpu.CompilerParams(
             collective_id=0, has_side_effects=True, vmem_limit_bytes=67043328
         ),
-    )(a, l)
+    )(a, l, left)
 
 
 def per_device(ancestor_inverse, factor, diag_inverse, widths, member):
@@ -260,18 +308,13 @@
         preferred_element_type=jnp.float32,
     )
     masked = factor * mask
-    product = grid_product(R, C, ancestor_inverse, masked)
-    offdiag = -product * mask
     if shard_cols == W:
         left = masked
     else:
         rows_full = lax.all_gather(masked, "col", axis=1, tiled=True)
         left = lax.dynamic_slice_in_dim(rows_full, col_start // W * W, W, 1)
-    local_gram = lax.dot_general(
-        left, product, (((0,), (0,)), ((), ())),
-        precision=lax.Precision.HIGH, preferred_element_type=jnp.float32,
-    )
-    gram = lax.psum_scatter(local_gram, "row", scatter_dimension=0, tiled=True)
+    product, gram = grid_product(R, C, ancestor_inverse, masked, left)
+    offdiag = -product * mask
     diag_rows = diag_inverse.shape[0]
     local_rows = my_row * diag_rows + jnp.arange(diag_rows, dtype=jnp.int32)
     inside = (local_rows[:, None] < width_col[None, :]) & col_keep[None, :]

time: 345 us -> 263 us (0.76)
  waiting for transfers between devices: 34.2 us -> 0 us
  Pallas kernels: 278 us -> 252 us
  between operations: 14.1 us -> 0.72 us
  matrix products: 10.2 us -> 3.95 us
    reduce_scatter x1 -> x0, waiting for transfers between devices: 34.2 us -> none  [per_device(): gram = lax.psum_scatter(local_gram, 'row', scatter_dimension=0, tiled=True)]
    pallas_call x1, Pallas kernels: 278 us -> 252 us  [grid_product(): pl.pallas_call(functools.partial(product_kernel, R, C), out_shape=[jax.Sh...]
    dot_general x1 -> x0, matrix products: 6.28 us -> none  [per_device(): lax.dot_general(left, product, (((0,), (0,)), ((), ())), precision=lax.Pr...]
  transfers between devices with their start and end apart: 1 -> 0, of which waited for: 1 -> 0; matrix products, arithmetic and copies ran while one was open for 1% -> 0% of each run, Pallas kernels for 0% -> 0%
where the time goes in v2:
time: 263 us
  Pallas kernels  252 us (96%)
  other arithmetic  5.81 us (2%)
  matrix products  3.95 us (2%)
    pallas_call x1, Pallas kernels, grid_product(): pl.pallas_call(functools.partial(product_kernel, R, C), out_shape=[jax.Sh...  252 us

profile of v2, /device:TPU:15, one launch (start us, length us, event | category | flops | bytes accessed | tf_op | source)
XLA Modules:
  0.0 262.9 jit_solution(15716666063984535590)
XLA Ops:
  0.6 0.6 iota_add_fusion.1
  1.2 0.7 select_reduce_fusion
  2.0 0.0 copy-start.2
  2.0 0.6 copy-done.2
  2.6 0.0 copy-start.4
  2.6 4.0 %bitcast_multiply_fusion.1 = (f32[768,640]{1,0:T(8,128)}, f32[640,768]{0,1:T(8,128)}) fusion(f32[768,640]{1,0:T(8,128)} %param.6, s32[4,768]{1,0:T(4,128)} %param.9, s32[640]{0:T(1024)S(1)} %add_select_fusion.2, pred[640]{0:T(1024)(128)(4,1)S(1)} %fusion.7), kind=kOutput, calls=%fused_computation.1 | convolution fusion | flops 4436992 | bytes 5913728 | tf_op jit(solution)/shard_map/dot_general | solution.py:306
  6.5 0.0 copy-done.4
  6.5 251.8 %shard_map.68 = (f32[768,640]{1,0:T(8,128)}, f32[80,640]{1,0:T(8,128)}) custom-call(f32[768,1536]{1,0:T(8,128)} %a_ref.1, f32[768,640]{1,0:T(8,128)} %get-tuple-element.6.l_ref.left_ref, f32[768,640]{1,0:T(8,128)} %get-tuple-element.6.l_ref.left_ref), custom_call_target="tpu_custom_call" | custom-call | tf_op jit(solution)/shard_map/pallas_call | solution.py:253
  258.4 0.0 copy-start
  258.4 0.0 copy-start.1
  258.4 0.0 copy-start.3
  258.4 0.0 copy-start.5
  258.4 0.0 copy-start.6
  258.4 3.7 %bitcast_multiply_fusion = f32[768,640]{1,0:T(8,128)} fusion(f32[640,768]{0,1:T(8,128)} %get-tuple-element.7, f32[768,640]{1,0:T(8,128)} %get-tuple-element.4), kind=kLoop, calls=%fused_computation | loop fusion | flops 983040 | bytes 5898240 | tf_op jit(solution)/shard_map/mul | solution.py:317
  262.1 0.0 copy-done
  262.1 0.0 copy-done.1
  262.1 0.0 copy-done.3
  262.1 0.0 copy-done.5
  262.1 0.0 copy-done.6
  262.1 0.8 add_select_fusion
  (2 shorter events, 0.0 us)
Async XLA Ops:
  2.0 0.6 copy-start.2
  2.6 4.0 %copy-start.4 = (pred[640]{0:T(1024)(128)(4,1)}, pred[640]{0:T(1024)(128)(4,1)S(1)}, u32[]{:S(2)}) copy-start(pred[640]{0:T(1024)(128)(4,1)S(1)} %fusion.7) | copy-start | bytes 1924
  258.4 3.7 %copy-start = (f32[80,640]{1,0:T(8,128)S(1)}, f32[80,640]{1,0:T(8,128)}, u32[]{:S(2)}) copy-start(f32[80,640]{1,0:T(8,128)} %param.7) | copy-start | bytes 614404
  258.4 3.7 %copy-start.1 = (f32[80,640]{1,0:T(8,128)S(1)}, f32[80,640]{1,0:T(8,128)}, u32[]{:S(2)}) copy-start(f32[80,640]{1,0:T(8,128)} %get-tuple-element.5) | copy-start | bytes 614404
  258.4 3.7 %copy-start.3 = (s32[640]{0:T(1024)S(1)}, s32[640]{0:T(1024)}, u32[]{:S(2)}) copy-start(s32[640]{0:T(1024)} %copy-done.2) | copy-start | bytes 7684
  258.4 3.7 %copy-start.5 = (pred[640]{0:T(1024)(128)(4,1)S(1)}, pred[640]{0:T(1024)(128)(4,1)}, u32[]{:S(2)}) copy-start(pred[640]{0:T(1024)(128)(4,1)} %copy-done.4) | copy-start | bytes 1924
  258.4 3.7 %copy-start.6 = (s32[80]{0:T(128)S(1)}, s32[80]{0:T(128)}, u32[]{:S(2)}) copy-start(s32[80]{0:T(128)} %iota_add_fusion.1) | copy-start | bytes 964

commit v3 on v2

--- a/solution.py
+++ b/solution.py
@@ -97,14 +97,37 @@
     for s, way in order:
         blocks.append(lax.rem(c + (s if way >= 0 else C - s), C))
 
-    def plane_copy(i, m):
-        ref = gath.at[blocks[i], g, mine]
-        return remote(ref, ref, s2.at[i, m - 1], r2.at[i, m - 1], lax.rem(j + m, C) * G + g, c)
-
-    def plane_wait(i, m):
-        from_j = lax.rem(j + C - m, C)
-        ref = gath.at[blocks[i], g, pl.ds(pl.multiple_of(from_j * chunk, chunk), chunk)]
-        remote(ref, ref, s2.at[i, m - 1], r2.at[i, m - 1], row, c).wait_recv()
+    relay = C == 4
+    near = (j + 1 - 2 * lax.rem(j, 2), lax.rem(j + 2, 4))
+    part_rows = chunk // 2
+
+    def place(m):
+        return lax.rem(j + m, C)
+
+    def source(m):
+        return lax.rem(j + C - m, C)
+
+    def piece_copy(i, k, owner, start, size, to):
+        at = pl.ds(pl.multiple_of(owner * chunk + start, 8), size)
+        ref = gath.at[blocks[i], g, at]
+        return remote(ref, ref, s2.at[i, k], r2.at[i, k], to * G + g, c)
+
+    def direct(i):
+        if relay:
+            return [piece_copy(i, k, j, 0, chunk, near[k]) for k in (0, 1)]
+        return [piece_copy(i, m - 1, j, 0, chunk, place(m)) for m in range(1, C)]
+
+    def direct_in(i):
+        if relay:
+            return [piece_copy(i, k, near[k], 0, chunk, j) for k in (0, 1)]
+        return [piece_copy(i, m - 1, source(m), 0, chunk, j) for m in range(1, C)]
+
+    def forward(i, k):
+        return piece_copy(i, 2 + k, near[k], k * part_rows, part_rows, near[1 - k])
+
+    def forward_in(i, k):
+        far = 3 - j
+        return piece_copy(i, 2 + k, far, k * part_rows, part_rows, j)
 
     def group_copy(i, n):
         ref = gath.at[blocks[i], g]
@@ -114,15 +137,19 @@
         ref = gath.at[blocks[i], lax.rem(g + G - n, G)]
         remote(ref, ref, s3.at[i, n - 1], r3.at[i, n - 1], row, c).wait_recv()
 
-    for i, (s, way) in enumerate(order):
+    def start_plane(i):
+        s, way = order[i]
         if s:
             m = C - s if way >= 0 else s
             ref = gath.at[blocks[i], g, mine]
             remote(ref, ref, s1.at[m - 1], r1.at[m - 1], row, c).wait_recv()
         else:
             keep.wait()
-        for m in range(1, C):
-            plane_copy(i, m).start()
+        for copy in direct(i):
+            copy.start()
+
+    start_plane(0)
+    start_plane(1)
 
     tb = row_tile(rows, 128)
     tm = row_tile(rows, 256)
@@ -169,8 +196,15 @@
 
     sends = []
     for i, (s, way) in enumerate(order):
-        for m in range(1, C):
-            plane_wait(i, m)
+        for k, copy in enumerate(direct_in(i)):
+            copy.wait_recv()
+            if relay:
+                forward(i, k).start()
+        if i + 2 < C:
+            start_plane(i + 2)
+        if relay:
+            for k in (0, 1):
+                forward_in(i, k).wait_recv()
         for n in range(1, G):
             group_copy(i, n).start()
         for n in range(1, G):
@@ -238,8 +272,8 @@
     for m in range(1, R):
         gram_copy(m).wait_send()
     for i in range(C):
-        for m in range(1, C):
-            plane_copy(i, m).wait_send()
+        for copy in direct(i) + ([forward(i, 0), forward(i, 1)] if relay else []):
+            copy.wait_send()
         for n in range(1, G):
             group_copy(i, n).wait_send()
 
@@ -273,8 +307,8 @@
             dma((C - 1,)),
             dma((C - 1,)),
             dma((C - 1,)),
-            dma((C, C - 1)),
-            dma((C, C - 1)),
+            dma((C, C)),
+            dma((C, C)),
             dma((C, max(G - 1, 1))),
             dma((C, max(G - 1, 1))),
             dma((2, C // 2)),

time: 263 us -> 267 us (1.015); the launches traced: 263 us -> 263 us
  no operation moved by 1% of the time
where the time goes in v3:
time: 267 us; the launch traced here: 263 us
  Pallas kernels  252 us (94%)
  other arithmetic  5.81 us (2%)
  matrix products  3.95 us (1%)
    pallas_call x1, Pallas kernels, grid_product(): pl.pallas_call(functools.partial(product_kernel, R, C), out_shape=[jax.Sh...  252 us

profile of v3, /device:TPU:15, one launch (start us, length us, event | category | flops | bytes accessed | tf_op | source)
XLA Modules:
  0.0 263.4 jit_solution(5807446166125617669)
XLA Ops:
  0.6 0.6 iota_add_fusion.1
  1.2 0.7 select_reduce_fusion
  2.0 0.0 copy-start.2
  2.0 0.6 copy-done.2
  2.6 0.0 copy-start.4
  2.6 4.0 %bitcast_multiply_fusion.1 = (f32[768,640]{1,0:T(8,128)}, f32[640,768]{0,1:T(8,128)}) fusion(f32[768,640]{1,0:T(8,128)} %param.6, s32[4,768]{1,0:T(4,128)} %param.9, s32[640]{0:T(1024)S(1)} %add_select_fusion.2, pred[640]{0:T(1024)(128)(4,1)S(1)} %fusion.7), kind=kOutput, calls=%fused_computation.1 | convolution fusion | flops 4436992 | bytes 5913728 | tf_op jit(solution)/shard_map/dot_general | solution.py:340
  6.5 0.0 copy-done.4
  6.5 252.3 %shard_map.68 = (f32[768,640]{1,0:T(8,128)}, f32[80,640]{1,0:T(8,128)}) custom-call(f32[768,1536]{1,0:T(8,128)} %a_ref.1, f32[768,640]{1,0:T(8,128)} %get-tuple-element.6.l_ref.left_ref, f32[768,640]{1,0:T(8,128)} %get-tuple-element.6.l_ref.left_ref), custom_call_target="tpu_custom_call" | custom-call | tf_op jit(solution)/shard_map/pallas_call | solution.py:287
  258.8 0.0 copy-start
  258.8 0.0 copy-start.1
  258.8 0.0 copy-start.3
  258.8 0.0 copy-start.5
  258.9 0.0 copy-start.6
  258.9 3.7 %bitcast_multiply_fusion = f32[768,640]{1,0:T(8,128)} fusion(f32[640,768]{0,1:T(8,128)} %get-tuple-element.7, f32[768,640]{1,0:T(8,128)} %get-tuple-element.4), kind=kLoop, calls=%fused_computation | loop fusion | flops 983040 | bytes 5898240 | tf_op jit(solution)/shard_map/mul | solution.py:351
  262.5 0.0 copy-done
  262.5 0.0 copy-done.1
  262.5 0.0 copy-done.3
  262.6 0.0 copy-done.5
  262.6 0.0 copy-done.6
  262.6 0.8 add_select_fusion
  (2 shorter events, 0.0 us)
Async XLA Ops:
  2.0 0.6 copy-start.2
  2.6 4.0 %copy-start.4 = (pred[640]{0:T(1024)(128)(4,1)}, pred[640]{0:T(1024)(128)(4,1)S(1)}, u32[]{:S(2)}) copy-start(pred[640]{0:T(1024)(128)(4,1)S(1)} %fusion.7) | copy-start | bytes 1924
  258.8 3.7 %copy-start = (f32[80,640]{1,0:T(8,128)S(1)}, f32[80,640]{1,0:T(8,128)}, u32[]{:S(2)}) copy-start(f32[80,640]{1,0:T(8,128)} %param.7) | copy-start | bytes 614404
  258.8 3.7 %copy-start.1 = (f32[80,640]{1,0:T(8,128)S(1)}, f32[80,640]{1,0:T(8,128)}, u32[]{:S(2)}) copy-start(f32[80,640]{1,0:T(8,128)} %get-tuple-element.5) | copy-start | bytes 614404
  258.8 3.7 %copy-start.3 = (s32[640]{0:T(1024)S(1)}, s32[640]{0:T(1024)}, u32[]{:S(2)}) copy-start(s32[640]{0:T(1024)} %copy-done.2) | copy-start | bytes 7684
  258.8 3.7 %copy-start.5 = (pred[640]{0:T(1024)(128)(4,1)S(1)}, pred[640]{0:T(1024)(128)(4,1)}, u32[]{:S(2)}) copy-start(pred[640]{0:T(1024)(128)(4,1)} %copy-done.4) | copy-start | bytes 1924
  258.9 3.7 %copy-start.6 = (s32[80]{0:T(128)S(1)}, s32[80]{0:T(128)}, u32[]{:S(2)}) copy-start(s32[80]{0:T(128)} %iota_add_fusion.1) | copy-start | bytes 964

commit v4 on v2

--- a/solution.py
+++ b/solution.py
@@ -89,10 +89,9 @@
         a_hi[at, pl.ds(0, depth)] = hi
         a_lo[at, pl.ds(0, depth)] = lo
 
-    order = [(half_ring, 0)]
+    order = [(0, 0), (half_ring, 0)]
     for s in range(half_ring - 1, 0, -1):
         order += [(s, -1), (s, 1)]
-    order += [(0, 0)]
     blocks = []
     for s, way in order:
         blocks.append(lax.rem(c + (s if way >= 0 else C - s), C))
@@ -196,7 +195,7 @@
     @pl.loop(0, rows // ta)
     def _(t):
         at = pl.ds(pl.multiple_of(t * ta, ta), ta)
-        x = part[C - 1, at, :] + recv[0, 0, at, :] + recv[1, 0, at, :]
+        x = part[0, at, :] + recv[0, 0, at, :] + recv[1, 0, at, :]
         out_ref[at, :] = x
         hi, lo = split(x)
         b_hi[at, :] = hi

time: 263 us -> 263 us (level)
  no operation moved by 1% of the time
where the time goes in v4:
time: 263 us
  Pallas kernels  252 us (96%)
  other arithmetic  5.81 us (2%)
  matrix products  3.95 us (2%)
    pallas_call x1, Pallas kernels, grid_product(): pl.pallas_call(functools.partial(product_kernel, R, C), out_shape=[jax.Sh...  252 us

profile of v4, /device:TPU:15, one launch (start us, length us, event | category | flops | bytes accessed | tf_op | source)
XLA Modules:
  0.0 262.7 jit_solution(3457299445760194051)
XLA Ops:
  0.6 0.6 iota_add_fusion.1
  1.2 0.7 select_reduce_fusion
  2.0 0.0 copy-start.2
  2.0 0.6 copy-done.2
  2.6 0.0 copy-start.4
  2.6 4.0 %bitcast_multiply_fusion.1 = (f32[768,640]{1,0:T(8,128)}, f32[640,768]{0,1:T(8,128)}) fusion(f32[768,640]{1,0:T(8,128)} %param.6, s32[4,768]{1,0:T(4,128)} %param.9, s32[640]{0:T(1024)S(1)} %add_select_fusion.2, pred[640]{0:T(1024)(128)(4,1)S(1)} %fusion.7), kind=kOutput, calls=%fused_computation.1 | convolution fusion | flops 4436992 | bytes 5913728 | tf_op jit(solution)/shard_map/dot_general | solution.py:305
  6.5 0.0 copy-done.4
  6.5 251.6 %shard_map.68 = (f32[768,640]{1,0:T(8,128)}, f32[80,640]{1,0:T(8,128)}) custom-call(f32[768,1536]{1,0:T(8,128)} %a_ref.1, f32[768,640]{1,0:T(8,128)} %get-tuple-element.6.l_ref.left_ref, f32[768,640]{1,0:T(8,128)} %get-tuple-element.6.l_ref.left_ref), custom_call_target="tpu_custom_call" | custom-call | tf_op jit(solution)/shard_map/pallas_call | solution.py:252
  258.2 0.0 copy-start
  258.2 0.0 copy-start.1
  258.2 0.0 copy-start.3
  258.2 0.0 copy-start.5
  258.2 0.0 copy-start.6
  258.2 3.7 %bitcast_multiply_fusion = f32[768,640]{1,0:T(8,128)} fusion(f32[640,768]{0,1:T(8,128)} %get-tuple-element.7, f32[768,640]{1,0:T(8,128)} %get-tuple-element.4), kind=kLoop, calls=%fused_computation | loop fusion | flops 983040 | bytes 5898240 | tf_op jit(solution)/shard_map/mul | solution.py:316
  261.9 0.0 copy-done
  261.9 0.0 copy-done.1
  261.9 0.0 copy-done.3
  261.9 0.0 copy-done.5
  261.9 0.0 copy-done.6
  261.9 0.8 add_select_fusion
  (2 shorter events, 0.0 us)
Async XLA Ops:
  2.0 0.6 copy-start.2
  2.6 4.0 %copy-start.4 = (pred[640]{0:T(1024)(128)(4,1)}, pred[640]{0:T(1024)(128)(4,1)S(1)}, u32[]{:S(2)}) copy-start(pred[640]{0:T(1024)(128)(4,1)S(1)} %fusion.7) | copy-start | bytes 1924
  258.2 3.7 %copy-start = (f32[80,640]{1,0:T(8,128)S(1)}, f32[80,640]{1,0:T(8,128)}, u32[]{:S(2)}) copy-start(f32[80,640]{1,0:T(8,128)} %param.7) | copy-start | bytes 614404
  258.2 3.7 %copy-start.1 = (f32[80,640]{1,0:T(8,128)S(1)}, f32[80,640]{1,0:T(8,128)}, u32[]{:S(2)}) copy-start(f32[80,640]{1,0:T(8,128)} %get-tuple-element.5) | copy-start | bytes 614404
  258.2 3.7 %copy-start.3 = (s32[640]{0:T(1024)S(1)}, s32[640]{0:T(1024)}, u32[]{:S(2)}) copy-start(s32[640]{0:T(1024)} %copy-done.2) | copy-start | bytes 7684
  258.2 3.7 %copy-start.5 = (pred[640]{0:T(1024)(128)(4,1)S(1)}, pred[640]{0:T(1024)(128)(4,1)}, u32[]{:S(2)}) copy-start(pred[640]{0:T(1024)(128)(4,1)} %copy-done.4) | copy-start | bytes 1924
  258.2 3.7 %copy-start.6 = (s32[80]{0:T(128)S(1)}, s32[80]{0:T(128)}, u32[]{:S(2)}) copy-start(s32[80]{0:T(128)} %iota_add_fusion.1) | copy-start | bytes 964
